TPU v7x, 32 devices: a whole 2x2x4 slice. The times are simulated.
32 devices in a mesh: dp: 16 (over z, y, core), tile: 2 (over x).
Axes of the slice: x: 2, y: 2, z: 4, core: 2. Of those that a mesh axis runs over, the one named last changes fastest.
Arguments:
- tokens: bfloat16 [16, 1024, 768], P('dp', 'tile'), may hold values from -11 to 11
- segment_ids: int32 [16, 1024], P('dp'), may hold values from 0 to 7, never falling along the last dimension, each value on 1 to 256 neighbouring positions
- keep_mask: int32 [16, 1024], P('dp'), may hold values 0 or 1
- gain_one: float32 [768], replicated, may hold values from 0.25 to 1.75
- bias_one: float32 [768], replicated, may hold values from -3 to 3
- qkv_weight: bfloat16 [768, 2304], replicated, may hold values from -0.21875 to 0.21875
- query_bias: float32 [768], replicated, may hold values from -3 to 3
- value_bias: float32 [768], replicated, may hold values from -3 to 3
- out_weight: bfloat16 [768, 768], replicated, may hold values from -2 to 2
- out_bias: float32 [768], replicated, may hold values from -3 to 3
- gain_two: float32 [768], replicated, may hold values from 0.25 to 1.75
- bias_two: float32 [768], replicated, may hold values from -3 to 3
- fc1_weight: bfloat16 [768, 3072], replicated, may hold values from -0.21875 to 0.21875
- fc1_bias: float32 [3072], replicated, may hold values from -3 to 3
- fc2_weight: bfloat16 [3072, 768], replicated, may hold values from -0.15625 to 0.15625
- fc2_bias: float32 [768], replicated, may hold values from -3 to 3
- cotangent: bfloat16 [16, 1024, 768], P('dp', 'tile'), may hold values from -6 to 6
Outputs:
- output: bfloat16 [16, 1024, 768], P('dp', 'tile')
- grad_tokens: bfloat16 [16, 1024, 768], P('dp', 'tile')
- gain_one_grad: float32 [768], replicated
- bias_one_grad: float32 [768], replicated
- qkv_grad: float32 [768, 2304], P('dp', 'tile')
- query_bias_grad: float32 [768], replicated
- value_bias_grad: float32 [768], replicated
- out_grad: float32 [768, 768], P('dp', 'tile')
- out_bias_grad: float32 [768], replicated
- gain_two_grad: float32 [768], replicated
- bias_two_grad: float32 [768], replicated
- fc1_grad: float32 [768, 3072], P('dp', 'tile')
- fc1_bias_grad: float32 [3072], replicated
- fc2_grad: float32 [3072, 768], P('dp', 'tile')
- fc2_bias_grad: float32 [768], replicated
- root_mean: float32 [4], replicated
Inputs may be any that keep to these rules, and one draw needn't show every extreme that they name: `segment_ids`: within a sequence the ids never fall; each of the 8 images has 1 to 256 slots, and one has exactly 256.
All inputs are finite; a program needn't handle non-finite values. No bound on the sum of `keep_mask` on one device may be relied on, other than what follows from the above.
Results may differ from a plain program's by a relative error of at most 0.017.
Values may be sent and summed in bfloat16 or wider, within the bound.
A program may use at most 192 MiB of HBM per device.

v0:
```python
import jax
import jax.numpy as jnp
from jax import lax
from jax.sharding import PartitionSpec as P

HEAD_DIM = 64


def layer_norm(values, norm_gain, norm_bias):
    average = jnp.mean(values, axis=-1, keepdims=True)
    centred = values - average
    variance = jnp.mean(centred * centred, axis=-1, keepdims=True)
    return centred * lax.rsqrt(variance + 1e-06) * norm_gain + norm_bias


def exact_gelu(values):
    return jax.nn.gelu(values, approximate=False)


def on_device(
    tokens,
    segment_ids,
    keep_mask,
    gain_one,
    bias_one,
    qkv_weight,
    query_bias,
    value_bias,
    out_weight,
    out_bias,
    gain_two,
    bias_two,
    fc1_weight,
    fc1_bias,
    fc2_weight,
    fc2_bias,
    cotangent,
):
    sequences, tile_rows, model_width = tokens.shape
    length = segment_ids.shape[1]
    count_rows = sequences * tile_rows
    head_block = 4 * HEAD_DIM
    score_scale = HEAD_DIM ** (-0.5)
    offset = lax.axis_index("tile") * tile_rows
    query_ids = lax.dynamic_slice_in_dim(segment_ids, offset, tile_rows, 1)
    query_keep = lax.dynamic_slice_in_dim(keep_mask, offset, tile_rows, 1)
    positions = offset + jnp.arange(tile_rows, dtype=jnp.int32)
    key_places = jnp.arange(length, dtype=jnp.int32)
    own_slot = positions[:, None] == key_places[None, :]
    usable = (keep_mask[:, None, :] == 1) | own_slot[None]
    allowed = ((query_ids[:, :, None] == segment_ids[:, None, :]) & usable)[:, None]
    flattened = tokens.reshape(count_rows, model_width).astype(jnp.float32)
    normed = layer_norm(flattened, gain_one, bias_one)
    normed_low = normed.astype(jnp.bfloat16)
    key_bias = jnp.zeros_like(query_bias)
    projected = jnp.dot(
        normed_low, qkv_weight, preferred_element_type=jnp.float32
    ) + jnp.concatenate([query_bias, key_bias, value_bias])
    projected_low = projected.astype(jnp.bfloat16).reshape(sequences, tile_rows, 3 * model_width)
    queries = projected_low[..., :model_width]
    shared_local = projected_low[..., model_width:]
    shared_all = lax.all_gather(shared_local, "tile", axis=1, tiled=True)
    keys_all = shared_all[..., :model_width]
    values_all = shared_all[..., model_width:]
    key_count = shared_all.shape[1]

    def split_heads(source, column):
        sliced = source[..., column : column + head_block]
        return sliced.reshape(sliced.shape[0], sliced.shape[1], 4, HEAD_DIM)

    def block_scores(query_part, key_part):
        scores = (
            jnp.einsum("sqhe,skhe->shqk", query_part, key_part, preferred_element_type=jnp.float32)
            * score_scale
        )
        return jnp.where(allowed, scores, -1e30)

    attended_parts = []
    logsums = []
    for column in range(0, model_width, head_block):
        masked = block_scores(split_heads(queries, column), split_heads(keys_all, column))
        row_peak = jnp.max(masked, axis=-1, keepdims=True)
        exponent = jnp.exp(masked - row_peak)
        row_total = jnp.sum(exponent, axis=-1, keepdims=True)
        softmax_probs = (exponent / row_total).astype(jnp.bfloat16)
        logsums.append(row_peak + jnp.log(row_total))
        attended_parts.append(
            jnp.einsum(
                "shqk,skhe->sqhe",
                softmax_probs,
                split_heads(values_all, column),
                preferred_element_type=jnp.float32,
            )
        )
    attended = jnp.concatenate(attended_parts, axis=2)
    attended_low = attended.reshape(count_rows, model_width).astype(jnp.bfloat16)
    branch_one = jnp.dot(attended_low, out_weight, preferred_element_type=jnp.float32) + out_bias
    hidden = flattened + branch_one
    normed_two = layer_norm(hidden, gain_two, bias_two)
    normed_two_low = normed_two.astype(jnp.bfloat16)
    inner = jnp.dot(normed_two_low, fc1_weight, preferred_element_type=jnp.float32) + fc1_bias
    active_low = exact_gelu(inner).astype(jnp.bfloat16)
    branch_two = jnp.dot(active_low, fc2_weight, preferred_element_type=jnp.float32) + fc2_bias
    result = hidden + branch_two
    output = result.astype(jnp.bfloat16).reshape(sequences, tile_rows, model_width)
    weighting = query_keep.reshape(count_rows, 1).astype(jnp.float32)
    squares = [
        jnp.sum(weighting * member * member)
        for member in (flattened, branch_one, branch_two, result)
    ]
    stats = jnp.stack(squares + [jnp.sum(weighting)])
    grad_result = cotangent.reshape(count_rows, model_width)
    fc2_grad = jnp.einsum("nf,nd->fd", active_low, grad_result, preferred_element_type=jnp.float32)
    fc2_bias_grad = jnp.sum(grad_result.astype(jnp.float32), axis=0)
    grad_active = jnp.einsum(
        "nd,fd->nf", grad_result, fc2_weight, preferred_element_type=jnp.float32
    )
    inner_value, gelu_back = jax.vjp(exact_gelu, inner)
    grad_inner_low = gelu_back(grad_active)[0].astype(jnp.bfloat16)
    fc1_grad = jnp.einsum(
        "nd,nf->df", normed_two_low, grad_inner_low, preferred_element_type=jnp.float32
    )
    fc1_bias_grad = jnp.sum(grad_inner_low.astype(jnp.float32), axis=0)
    grad_normed_two = jnp.einsum(
        "nf,df->nd", grad_inner_low, fc1_weight, preferred_element_type=jnp.float32
    )
    normed_again, norm_back_two = jax.vjp(layer_norm, hidden, gain_two, bias_two)
    grad_hidden_part, gain_two_grad, bias_two_grad = norm_back_two(grad_normed_two)
    grad_hidden = grad_result.astype(jnp.float32) + grad_hidden_part
    grad_branch_low = grad_hidden.astype(jnp.bfloat16)
    out_grad = jnp.einsum(
        "nd,ne->de", attended_low, grad_branch_low, preferred_element_type=jnp.float32
    )
    out_bias_grad = jnp.sum(grad_branch_low.astype(jnp.float32), axis=0)
    grad_attended_low = (
        jnp.einsum("ne,de->nd", grad_branch_low, out_weight, preferred_element_type=jnp.float32)
        .astype(jnp.bfloat16)
        .reshape(sequences, tile_rows, model_width)
    )
    query_grads = []
    key_grads = []
    value_grads = []
    for block_index, column in enumerate(range(0, model_width, head_block)):
        query_part = split_heads(queries, column)
        key_part = split_heads(keys_all, column)
        value_part = split_heads(values_all, column)
        grad_part = split_heads(grad_attended_low, column)
        masked = block_scores(query_part, key_part)
        probs_again = jnp.exp(masked - logsums[block_index])
        grad_probs = jnp.einsum(
            "sqhe,skhe->shqk", grad_part, value_part, preferred_element_type=jnp.float32
        )
        centre = jnp.sum(probs_again * grad_probs, axis=-1, keepdims=True)
        grad_scores = (probs_again * (grad_probs - centre)).astype(jnp.bfloat16)
        query_grads.append(
            jnp.einsum("shqk,skhe->sqhe", grad_scores, key_part, preferred_element_type=jnp.float32)
            * score_scale
        )
        key_grads.append(
            jnp.einsum(
                "shqk,sqhe->skhe", grad_scores, query_part, preferred_element_type=jnp.float32
            )
            * score_scale
        )
        value_grads.append(
            jnp.einsum(
                "shqk,sqhe->skhe",
                probs_again.astype(jnp.bfloat16),
                grad_part,
                preferred_element_type=jnp.float32,
            )
        )
    grad_query = jnp.concatenate(query_grads, axis=2).reshape(sequences, tile_rows, model_width)
    grad_key_full = jnp.concatenate(key_grads, axis=2).reshape(sequences, key_count, model_width)
    grad_value_full = jnp.concatenate(value_grads, axis=2).reshape(
        sequences, key_count, model_width
    )
    grad_shared_full = jnp.concatenate([grad_key_full, grad_value_full], axis=-1)
    grad_shared = lax.psum_scatter(
        grad_shared_full.astype(jnp.bfloat16), "tile", scatter_dimension=1, tiled=True
    ).astype(jnp.float32)
    grad_projected_low = (
        jnp.concatenate([grad_query, grad_shared], axis=-1)
        .astype(jnp.bfloat16)
        .reshape(count_rows, 3 * model_width)
    )
    qkv_grad = jnp.einsum(
        "nd,ne->de", normed_low, grad_projected_low, preferred_element_type=jnp.float32
    )
    column_sums = jnp.sum(grad_projected_low.astype(jnp.float32), axis=0)
    query_bias_grad = column_sums[:model_width]
    value_bias_grad = column_sums[2 * model_width :]
    grad_normed = jnp.einsum(
        "ne,de->nd", grad_projected_low, qkv_weight, preferred_element_type=jnp.float32
    )
    normed_first, norm_back_one = jax.vjp(layer_norm, flattened, gain_one, bias_one)
    grad_tokens_part, gain_one_grad, bias_one_grad = norm_back_one(grad_normed)
    grad_tokens = (
        (grad_hidden + grad_tokens_part)
        .astype(jnp.bfloat16)
        .reshape(sequences, tile_rows, model_width)
    )
    totals_small = lax.psum(
        (
            gain_one_grad,
            bias_one_grad,
            query_bias_grad,
            value_bias_grad,
            out_bias_grad,
            gain_two_grad,
            bias_two_grad,
            fc1_bias_grad,
            fc2_bias_grad,
            stats,
        ),
        ("dp", "tile"),
    )
    matrices = (qkv_grad, out_grad, fc1_grad, fc2_grad)
    row_shares = (
        lax.psum_scatter(
            matrices[0].astype(jnp.bfloat16), "dp", scatter_dimension=0, tiled=True
        ).astype(jnp.float32),
        lax.psum_scatter(
            matrices[1].astype(jnp.bfloat16), "dp", scatter_dimension=0, tiled=True
        ).astype(jnp.float32),
        lax.psum_scatter(
            matrices[2].astype(jnp.bfloat16), "dp", scatter_dimension=0, tiled=True
        ).astype(jnp.float32),
        lax.psum_scatter(
            matrices[3].astype(jnp.bfloat16), "dp", scatter_dimension=0, tiled=True
        ).astype(jnp.float32),
    )
    reduced = (
        lax.psum_scatter(
            row_shares[0].astype(jnp.bfloat16), "tile", scatter_dimension=1, tiled=True
        ).astype(jnp.float32),
        lax.psum_scatter(
            row_shares[1].astype(jnp.bfloat16), "tile", scatter_dimension=1, tiled=True
        ).astype(jnp.float32),
        lax.psum_scatter(
            row_shares[2].astype(jnp.bfloat16), "tile", scatter_dimension=1, tiled=True
        ).astype(jnp.float32),
        lax.psum_scatter(
            row_shares[3].astype(jnp.bfloat16), "tile", scatter_dimension=1, tiled=True
        ).astype(jnp.float32),
    )
    totals = totals_small[9]
    root_mean = jnp.sqrt(totals[:4] / (totals[4] * model_width))
    return (
        output,
        grad_tokens,
        totals_small[0],
        totals_small[1],
        reduced[0],
        totals_small[2],
        totals_small[3],
        reduced[1],
        totals_small[4],
        totals_small[5],
        totals_small[6],
        reduced[2],
        totals_small[7],
        reduced[3],
        totals_small[8],
        root_mean,
    )


def solution(mesh):
    placed = (
        P("dp", "tile", None),
        P("dp", None),
        P("dp", None),
        P(),
        P(),
        P(),
        P(),
        P(),
        P(),
        P(),
        P(),
        P(),
        P(),
        P(),
        P(),
        P(),
        P("dp", "tile", None),
    )
    return jax.shard_map(
        on_device,
        mesh=mesh,
        in_specs=placed,
        out_specs=(
            P("dp", "tile", None),
            P("dp", "tile", None),
            P(),
            P(),
            P("dp", "tile"),
            P(),
            P(),
            P("dp", "tile"),
            P(),
            P(),
            P(),
            P("dp", "tile"),
            P(),
            P("dp", "tile"),
            P(),
            P(),
        ),
        check_vma=False,
    )
```

profile of v0, /device:TPU:0, one launch (start us, length us, event | category | flops | bytes accessed | tf_op | source)
XLA Modules:
  0.0 602.2 jit_solution(12091611203027383656)
XLA Ops:
  11.5 3.3 fusion.25
  17.7 2.0 fusion.106
  27.8 37.7 %all-gather.2.cloned.1.call-done = bf16[1,1024,1536]{2,1,0:T(8,128)(2,1)} async-done(((bf16[1,512,1536]{2,1,0:T(8,128)(2,1)}), bf16[1,1024,1536]{2,1,0:T(8,128)(2,1)}) %all-gather.2.cloned.1.call-update) | async-done | bytes 3145744 | tf_op jit(solution)/shard_map/all_gather | solution.py:62
  65.4 3.6 fusion.105
  69.0 2.0 copy.71
  71.0 2.1 copy.77
  73.1 2.0 copy.75
  75.1 2.0 copy.74
  77.2 2.1 copy.72
  79.2 2.1 copy.69
  81.3 3.1 fusion.110
  84.4 2.0 fusion.1
  86.5 2.1 fusion.80
  92.4 2.1 fusion.81
  99.6 2.1 fusion.79
  101.9 2.0 fusion.103
  104.3 21.1 %multiply_convert_fusion.3 = (bf16[512,3072]{1,0:T(8,128)(2,1)}, f32[512,3072]{1,0:T(8,128)}, f32[512,3072]{1,0:T(8,128)}) fusion(f32[3072]{0:T(1024)S(1)} %copy-done.61, bf16[768,3072]{1,0:T(8,128)(2,1)S(1)} %bitcast.237, f32[512,768]{1,0:T(8,128)S(1)} %get-tuple-element.48, f32[768]{0:T(1024)S(1)} %copy-done.63, f32[768]{0:T(1024)S(1)} %copy-done.58, ...), kind=kOutput, calls=%fused_computation.28 | convolution fusion | flops 2521694208 | bytes 22042624 | tf_op jit(solution)/shard_map/dot_general | solution.py:101
  125.4 8.6 %convert_reduce_fusion = (f32[3072]{0:T(1024)}, bf16[512,3072]{1,0:T(8,128)(2,1)S(1)}) fusion(f32[512,3072]{1,0:T(8,128)} %get-tuple-element.46, bf16[3072,768]{1,0:T(8,128)(2,1)S(1)} %bitcast.239, bf16[1,512,768]{2,1,0:T(8,128)(2,1)S(1)} %copy-done.23, f32[512,3072]{1,0:T(8,128)} %get-tuple-element.73, f32[3072]{0:T(1024)S(1)} %copy-done.61), kind=kOutput, calls=%fused_computation.26 | convolution fusion | flops 2442654720 | bytes 21258240 | tf_op jit(solution)/shard_map/nd,fd->nf/dot_general | solution.py:115
  134.0 2.7 fusion.112
  137.1 4.8 fusion.44
  147.3 2.3 fusion.57
  152.4 5.7 fusion.67
  158.1 7.0 %multiply_reduce_fusion.2 = (f32[4,512]{1,0:T(4,128)}, f32[4,512,1024]{2,1,0:T(8,128)}) fusion(f32[4,512,1024]{2,1,0:T(8,128)} %copy-done.3, f32[4,512]{1,0:T(4,128)S(1)} %copy-done.39, bf16[512,4,64]{0,2,1:T(8,128)(2,1)S(1)} %bitcast.212, bf16[1024,4,64]{0,2,1:T(8,128)(2,1)S(1)} %bitcast.223), kind=kOutput, calls=%fused_computation.8 | convolution fusion | flops 274724864 | bytes 17580032 | tf_op jit(solution)/shard_map/sqhe,skhe->shqk/dot_general | solution.py:150
  166.9 5.8 fusion.61
  172.7 7.2 %multiply_reduce_fusion = (f32[4,512]{1,0:T(4,128)}, f32[4,512,1024]{2,1,0:T(8,128)}) fusion(f32[4,512,1024]{2,1,0:T(8,128)} %copy-done.2, f32[4,512]{1,0:T(4,128)S(1)} %log_add_fusion, bf16[512,4,64]{0,2,1:T(8,128)(2,1)S(1)} %bitcast.214, bf16[1024,4,64]{0,2,1:T(8,128)(2,1)S(1)} %bitcast.221), kind=kOutput, calls=%fused_computation.2 | convolution fusion | flops 274724864 | bytes 17580032 | tf_op jit(solution)/shard_map/sqhe,skhe->shqk/dot_general | solution.py:150
  181.7 5.8 fusion.64
  187.6 7.0 %multiply_reduce_fusion.1 = (f32[4,512]{1,0:T(4,128)}, f32[4,512,1024]{2,1,0:T(8,128)}) fusion(f32[4,512,1024]{2,1,0:T(8,128)} %copy-done.1, f32[4,512]{1,0:T(4,128)S(1)} %log_add_fusion.1, bf16[512,4,64]{0,2,1:T(8,128)(2,1)S(1)} %bitcast.216, bf16[1024,4,64]{0,2,1:T(8,128)(2,1)S(1)} %bitcast.219), kind=kOutput, calls=%fused_computation.5 | convolution fusion | flops 274724864 | bytes 17580032 | tf_op jit(solution)/shard_map/sqhe,skhe->shqk/dot_general | solution.py:150
  194.7 7.0 %multiply_convert_fusion.2 = bf16[4,512,1024]{2,1,0:T(8,128)(2,1)S(1)} fusion(f32[4,512,1024]{2,1,0:T(8,128)} %get-tuple-element.79, f32[4,512,1024]{2,1,0:T(8,128)} %copy-done.3, f32[4,512]{1,0:T(4,128)} %get-tuple-element.78, f32[4,512]{1,0:T(4,128)} %log_add_fusion.2), kind=kLoop, calls=%fused_computation.7 | loop fusion | flops 8388608 | bytes 20987904 | tf_op jit(solution)/shard_map/convert_element_type | solution.py:154
  204.5 4.9 multiply_convert_fusion
  212.3 4.4 multiply_convert_fusion.1
  218.7 1.9 pad_maximum_fusion
  220.7 32.2 %reduce-scatter.20.cloned.1.call-done = bf16[48,768]{1,0:T(8,128)(2,1)} async-done(((bf16[768,768]{1,0:T(8,128)(2,1)}), bf16[48,768]{1,0:T(8,128)(2,1)}) %reduce-scatter.20.cloned.1.call-update) | async-done | bytes 73744 | tf_op jit(solution)/shard_map/reduce_scatter | solution.py:223
  254.7 7.2 %convolution_convert_fusion = bf16[3072,768]{1,0:T(8,128)(2,1)} fusion(bf16[512,3072]{1,0:T(8,128)(2,1)} %get-tuple-element.45, bf16[1,512,768]{2,1,0:T(8,128)(2,1)} %param.33), kind=kOutput, calls=%fused_computation.42 | convolution fusion | flops 2418278400 | bytes 8650752 | tf_op jit(solution)/shard_map/nf,nd->fd/dot_general | solution.py:113
  262.6 7.4 %convolution_convert_fusion.1 = bf16[768,3072]{1,0:T(8,128)(2,1)} fusion(bf16[512,3072]{1,0:T(8,128)(2,1)} %copy-done.66, f32[512,768]{1,0:T(8,128)} %copy-done.11, f32[768]{0:T(1024)S(1)} %copy-done.64, f32[768]{0:T(1024)S(1)} %copy-done.59, f32[512]{0:T(512)S(1)} %copy-done.56, f32[512]{0:T(512)S(1)} %copy-done.49), kind=kOutput, calls=%fused_computation.43 | convolution fusion | flops 2420244480 | bytes 9447424 | tf_op jit(solution)/shard_map/nd,nf->df/dot_general | solution.py:120
  270.1 3.9 fusion.78
  274.1 2.6 fusion.76
  279.1 18.5 %reduce-scatter.16.cloned.1.call-done = bf16[1,512,1536]{1,2,0:T(8,128)(2,1)} async-done(((bf16[1,1024,1536]{1,2,0:T(8,128)(2,1)}), bf16[1,512,1536]{1,2,0:T(8,128)(2,1)}) %reduce-scatter.16.cloned.1.call-update) | async-done | bytes 1572880 | tf_op jit(solution)/shard_map/reduce_scatter | solution.py:179
  297.5 6.0 convolution_convert_fusion.2
  303.6 7.7 %reduce-scatter.30.cloned.1.call-done = bf16[384,48]{1,0:T(8,128)(2,1)} async-done(((bf16[768,48]{1,0:T(8,128)(2,1)}), bf16[384,48]{1,0:T(8,128)(2,1)}) %reduce-scatter.30.cloned.1.call-update) | async-done | bytes 36880
  314.2 76.8 %reduce-scatter.26.cloned.1.call-done = bf16[192,768]{1,0:T(8,128)(2,1)} async-done(((bf16[3072,768]{1,0:T(8,128)(2,1)}), bf16[192,768]{1,0:T(8,128)(2,1)}) %reduce-scatter.26.cloned.1.call-update) | async-done | bytes 294928 | tf_op jit(solution)/shard_map/reduce_scatter | solution.py:229
  393.0 5.6 fusion.98
  401.2 68.2 %reduce-scatter.22.cloned.1.call-done = bf16[48,3072]{1,0:T(8,128)(2,1)} async-done(((bf16[768,3072]{1,0:T(8,128)(2,1)}), bf16[48,3072]{1,0:T(8,128)(2,1)}) %reduce-scatter.22.cloned.1.call-update) | async-done | bytes 294928 | tf_op jit(solution)/shard_map/reduce_scatter | solution.py:226
  469.7 2.0 convert_reduce_fusion.1
  471.7 3.8 stack.23
  476.1 4.8 convert_reduce_fusion.2
  480.9 59.9 %reduce-scatter.18.cloned.1.call-done = bf16[48,2304]{1,0:T(8,128)(2,1)} async-done(((bf16[768,2304]{1,0:T(8,128)(2,1)}), bf16[48,2304]{1,0:T(8,128)(2,1)}) %reduce-scatter.18.cloned.1.call-update) | async-done | bytes 221200 | tf_op jit(solution)/shard_map/reduce_scatter | solution.py:220
  540.9 2.0 copy.81
  543.5 41.5 %all-reduce = (f32[768]{0:T(1024)}, f32[768]{0:T(1024)}, f32[768]{0:T(1024)}, f32[768]{0:T(1024)}, f32[768]{0:T(1024)}, /*index=5*/f32[768]{0:T(1024)}, f32[768]...) all-reduce(f32[768]{0:T(1024)} %get-tuple-element.18, ...), channel_id=1, replica_groups=mesh['dp'=16,'tile'=2] {'dp','tile'}, use_global_device_ids=true, to_apply=%region_19.20 | all-reduce | flops 9221 | bytes 73768 | tf_op jit(solution)/shard_map/psum | solution.py:203
  (236 shorter events, 67.5 us)
Async XLA Ops:
  7.2 4.3 copy-start
  7.2 58.2 %all-gather.2.cloned.1.call-start = ((), (), s32[]{:S(2)}) async-start(), calls=%async_computation.9 | async-start | bytes 4718592 | tf_op jit(solution)/shard_map/all_gather | solution.py:62
  8.7 6.1 %copy-start.42 = (f32[512]{0:T(512)}, f32[512]{0:T(512)S(1)}, u32[]{:S(2)}) copy-start(f32[512]{0:T(512)S(1)} %broadcast_multiply_fusion.1) | copy-start | bytes 6148
  10.2 4.6 copy-start.45
  16.3 8.8 %copy-start.53 = (s32[1,1024]{1,0:T(1,128)S(1)}, s32[1,1024]{1,0:T(1,128)}, u32[]{:S(2)}) copy-start(s32[1,1024]{1,0:T(1,128)} %param.18) | copy-start | bytes 12292
  16.3 8.8 %copy-start.54 = (s32[1,1024]{1,0:T(1,128)S(1)}, s32[1,1024]{1,0:T(1,128)}, u32[]{:S(2)}) copy-start(s32[1,1024]{1,0:T(1,128)} %param.19) | copy-start | bytes 12292
  17.6 235.3 %reduce-scatter.20.cloned.1.call-start = ((), (), s32[]{:S(2)}) async-start(), calls=%async_computation.12 | async-start | bytes 1253376 | tf_op jit(solution)/shard_map/reduce_scatter | solution.py:223
  84.4 4.3 copy-start.1
  90.5 4.1 copy-start.2
  96.5 5.2 copy-start.3
  99.5 4.7 slice-start.4
  99.5 4.7 slice-start.5
  101.9 23.5 %slice-start.6 = ((s8[4718592]{0:T(1024)(128)(4,1)}), s8[4194304]{0:T(1024)(128)(4,1)S(1)}, s32[]{:S(2)}) async-start(s8[4718592]{0:T(1024)(128)(4,1)} %bitcast.238), calls=%async_computation.25 | async-start | bytes 8388608
  103.9 38.0 %copy-start.11 = (f32[512,768]{1,0:T(8,128)}, f32[512,768]{1,0:T(8,128)S(1)}, u32[]{:S(2)}) copy-start(f32[512,768]{1,0:T(8,128)S(1)} %get-tuple-element.48) | copy-start | bytes 4718596
  103.9 38.0 %copy-start.48 = (f32[512]{0:T(512)}, f32[512]{0:T(512)S(1)}, u32[]{:S(2)}) copy-start(f32[512]{0:T(512)S(1)} %broadcast_multiply_fusion) | copy-start | bytes 6148
  104.3 37.6 %copy-start.55 = (f32[512]{0:T(512)}, f32[512]{0:T(512)S(1)}, u32[]{:S(2)}) copy-start(f32[512]{0:T(512)S(1)} %fusion.91) | copy-start | bytes 6148
  104.3 21.1 %copy-start.23 = (bf16[1,512,768]{2,1,0:T(8,128)(2,1)S(1)}, bf16[1,512,768]{2,1,0:T(8,128)(2,1)}, u32[]{:S(2)}) copy-start(bf16[1,512,768]{2,1,0:T(8,128)(2,1)} %param.33) | copy-start | bytes 2359300
  104.3 21.1 %slice-start.7 = ((s8[4718592]{0:T(1024)(128)(4,1)}), s8[524288]{0:T(1024)(128)(4,1)S(1)}, s32[]{:S(2)}) async-start(s8[4718592]{0:T(1024)(128)(4,1)} %bitcast.238), calls=%async_computation.26 | async-start | bytes 1048576
  152.3 5.7 copy-start.24
  152.3 5.7 copy-start.33
  152.4 5.7 copy-start.39
  166.9 5.8 copy-start.25
  166.9 5.8 copy-start.31
  181.7 5.8 copy-start.26
  181.7 5.8 copy-start.29
  194.6 102.9 %reduce-scatter.16.cloned.1.call-start = ((), (), s32[]{:S(2)}) async-start(), calls=%async_computation.10 | async-start | bytes 4718592 | tf_op jit(solution)/shard_map/reduce_scatter | solution.py:179
  194.7 9.1 %slice-start.2 = ((s8[8388608]{0:T(1024)(128)(4,1)}), s8[4194304]{0:T(1024)(128)(4,1)S(1)}, s32[]{:S(2)}) async-start(s8[8388608]{0:T(1024)(128)(4,1)} %bitcast.190), calls=%async_computation.21 | async-start | bytes 8388608
  194.7 7.0 %copy-start.22 = (bf16[1,512,256]{1,2,0:T(8,128)(2,1)S(1)}, bf16[1,512,256]{1,2,0:T(8,128)(2,1)}, u32[]{:S(2)}) copy-start(bf16[1,512,256]{1,2,0:T(8,128)(2,1)} %copy.70) | copy-start | bytes 786436
  194.7 9.8 %slice-start.3 = ((s8[8388608]{0:T(1024)(128)(4,1)}), s8[4194304]{0:T(1024)(128)(4,1)S(1)}, s32[]{:S(2)}) async-start(s8[8388608]{0:T(1024)(128)(4,1)} %bitcast.190), calls=%async_computation.22 | async-start | bytes 8388608
  203.8 8.5 %slice-start = ((s8[8388608]{0:T(1024)(128)(4,1)}), s8[4194304]{0:T(1024)(128)(4,1)S(1)}, s32[]{:S(2)}) async-start(s8[8388608]{0:T(1024)(128)(4,1)} %bitcast.188), calls=%async_computation.19 | async-start | bytes 8388608
  204.5 4.9 copy-start.20
  204.5 7.8 %slice-start.1 = ((s8[8388608]{0:T(1024)(128)(4,1)}), s8[4194304]{0:T(1024)(128)(4,1)S(1)}, s32[]{:S(2)}) async-start(s8[8388608]{0:T(1024)(128)(4,1)} %bitcast.188), calls=%async_computation.20 | async-start | bytes 8388608
  212.3 4.4 copy-start.18
  220.7 90.6 %reduce-scatter.30.cloned.1.call-start = ((), (), s32[]{:S(2)}) async-start(), calls=%async_computation.17 | async-start | bytes 294912
  254.6 136.4 %reduce-scatter.26.cloned.1.call-start = ((), (), s32[]{:S(2)}) async-start(), calls=%async_computation.15 | async-start | bytes 5013504 | tf_op jit(solution)/shard_map/reduce_scatter | solution.py:229
  261.9 207.5 %reduce-scatter.22.cloned.1.call-start = ((), (), s32[]{:S(2)}) async-start(), calls=%async_computation.13 | async-start | bytes 5013504 | tf_op jit(solution)/shard_map/reduce_scatter | solution.py:226
  270.0 270.9 %reduce-scatter.18.cloned.1.call-start = ((), (), s32[]{:S(2)}) async-start(), calls=%async_computation.11 | async-start | bytes 3760128 | tf_op jit(solution)/shard_map/reduce_scatter | solution.py:220
  270.0 6.7 %copy-start.8 = (bf16[4,512,1024]{2,1,0:T(8,128)(2,1)S(1)}, bf16[4,512,1024]{2,1,0:T(8,128)(2,1)}, u32[]{:S(2)}) copy-start(bf16[4,512,1024]{2,1,0:T(8,128)(2,1)} %copy-done.7) | copy-start | bytes 12582916
  270.0 6.6 %copy-start.17 = (bf16[1,1024,256]{1,2,0:T(8,128)(2,1)S(1)}, bf16[1,1024,256]{1,2,0:T(8,128)(2,1)}, u32[]{:S(2)}) copy-start(bf16[1,1024,256]{1,2,0:T(8,128)(2,1)} %copy.74) | copy-start | bytes 1572868
  274.0 23.5 %copy-start.43 = (f32[512]{0:T(512)S(1)}, f32[512]{0:T(512)}, u32[]{:S(2)}) copy-start(f32[512]{0:T(512)} %copy-done.42) | copy-start | bytes 6148
  274.0 23.5 %copy-start.46 = (f32[512]{0:T(512)S(1)}, f32[512]{0:T(512)}, u32[]{:S(2)}) copy-start(f32[512]{0:T(512)} %copy-done.45) | copy-start | bytes 6148
  274.0 23.5 %copy-start.52 = (f32[768]{0:T(1024)S(1)}, f32[768]{0:T(1024)}, u32[]{:S(2)}) copy-start(f32[768]{0:T(1024)} %param.20) | copy-start | bytes 9220
  274.0 23.5 %copy-start.65 = (f32[768]{0:T(1024)S(1)}, f32[768]{0:T(1024)}, u32[]{:S(2)}) copy-start(f32[768]{0:T(1024)} %param.21) | copy-start | bytes 9220
  303.5 283.2 %reduce-scatter.32.cloned.1.call-start = ((), (), s32[]{:S(2)}) async-start(), calls=%async_computation.18 | async-start | bytes 589824
  392.9 197.2 %reduce-scatter.24.cloned.1.call-start = ((), (), s32[]{:S(2)}) async-start(), calls=%async_computation.14 | async-start | bytes 442368 | tf_op jit(solution)/shard_map/reduce_scatter | solution.py:240
  393.0 5.6 copy-start.51
  393.0 6.8 %copy-start.10 = (bf16[1,512,768]{2,1,0:T(8,128)(2,1)S(1)}, bf16[1,512,768]{2,1,0:T(8,128)(2,1)}, u32[]{:S(2)}) copy-start(bf16[1,512,768]{2,1,0:T(8,128)(2,1)} %param.17) | copy-start | bytes 2359300
  469.4 122.3 %reduce-scatter.28.cloned.1.call-start = ((), (), s32[]{:S(2)}) async-start(), calls=%async_computation.16 | async-start | bytes 884736
  (38 other events, 77.4 us)
Sparse Core Ops, SparseCore 0:
  17.8 47.6 all-gather.1
  194.7 58.1 reduce-scatter.19
  255.1 42.3 reduce-scatter.15
  300.3 10.9 reduce-scatter.29
  315.4 75.5 reduce-scatter.25
  394.7 74.5 reduce-scatter.21
  473.7 67.0 reduce-scatter.17
  543.2 12.3 reduce-scatter.31
  557.8 11.9 reduce-scatter.23
  571.9 15.7 reduce-scatter.27
where the time goes:
time: 609 us; the launch traced here: 602 us
  waiting for transfers between devices  301 us (49%)
  matrix products  135 us (22%)
  local copies, waits for them, and re-layouts  57.3 us (9%)
  other arithmetic  50.4 us (8%)
  blocking collectives  41.5 us (7%)
  between operations  16 us (3%)
    reduce_scatter x1, waiting for transfers between devices, on_device(): lax.psum_scatter(matrices[3].astype(jnp.bfloat16), 'dp', scatter_dimensio...  76.8 us
    reduce_scatter x1, waiting for transfers between devices, on_device(): lax.psum_scatter(matrices[2].astype(jnp.bfloat16), 'dp', scatter_dimensio...  68.2 us
    reduce_scatter x1, waiting for transfers between devices, on_device(): lax.psum_scatter(matrices[0].astype(jnp.bfloat16), 'dp', scatter_dimensio...  59.9 us
    psum x1, blocking collectives, on_device(): lax.psum((gain_one_grad, bias_one_grad, query_bias_grad, value_bias_grad,...  41.5 us
    all_gather x1, waiting for transfers between devices, on_device(): shared_all = lax.all_gather(shared_local, 'tile', axis=1, tiled=True)  37.7 us
    reduce_scatter x1, waiting for transfers between devices, on_device(): lax.psum_scatter(matrices[1].astype(jnp.bfloat16), 'dp', scatter_dimensio...  32.2 us
    slice x15, local copies, waits for them, and re-layouts, split_heads(): sliced = source[..., column:column + head_block]  29.6 us
    unnamed x158, local copies, waits for them, and re-layouts  21.5 us
  transfers between devices with their start and end apart: 10, of which 7 were waited for; matrix products, arithmetic and copies ran while one was open for 16% of the time, Pallas kernels for 0%

commit v1 on v0

--- a/solution.py
+++ b/solution.py
@@ -200,7 +200,7 @@
         .astype(jnp.bfloat16)
         .reshape(sequences, tile_rows, model_width)
     )
-    totals_small = lax.psum(
+    partial = lax.psum(
         (
             gain_one_grad,
             bias_one_grad,
@@ -213,8 +213,9 @@
             fc2_bias_grad,
             stats,
         ),
-        ("dp", "tile"),
-    )
+        "tile",
+    )
+    totals_small = lax.psum(partial, "dp")
     matrices = (qkv_grad, out_grad, fc1_grad, fc2_grad)
     row_shares = (
         lax.psum_scatter(

time: 609 us -> 637 us (1.046)
  blocking collectives: 41.5 us -> 69.4 us
    psum x0 -> x1, blocking collectives: none -> 58.8 us  [on_device(): totals_small = lax.psum(partial, 'dp')]
    psum x1, blocking collectives: 41.5 us -> 10.6 us  [on_device(): lax.psum((gain_one_grad, bias_one_grad, query_bias_grad, value_bias_grad,...]
  transfers between devices with their start and end apart: 10 -> 10, of which waited for: 7 -> 7; matrix products, arithmetic and copies ran while one was open for 16% -> 15% of each run, Pallas kernels for 0% -> 0%
where the time goes in v1:
time: 637 us; the launch traced here: 630 us
  waiting for transfers between devices  301 us (47%)
  matrix products  135 us (21%)
  blocking collectives  69.4 us (11%)
  local copies, waits for them, and re-layouts  57.4 us (9%)
  other arithmetic  50.5 us (8%)
  between operations  16 us (3%)
    reduce_scatter x1, waiting for transfers between devices, on_device(): lax.psum_scatter(matrices[3].astype(jnp.bfloat16), 'dp', scatter_dimensio...  76.8 us
    reduce_scatter x1, waiting for transfers between devices, on_device(): lax.psum_scatter(matrices[2].astype(jnp.bfloat16), 'dp', scatter_dimensio...  68.2 us
    reduce_scatter x1, waiting for transfers between devices, on_device(): lax.psum_scatter(matrices[0].astype(jnp.bfloat16), 'dp', scatter_dimensio...  59.8 us
    psum x1, blocking collectives, on_device(): totals_small = lax.psum(partial, 'dp')  58.8 us
    all_gather x1, waiting for transfers between devices, on_device(): shared_all = lax.all_gather(shared_local, 'tile', axis=1, tiled=True)  37.6 us
    reduce_scatter x1, waiting for transfers between devices, on_device(): lax.psum_scatter(matrices[1].astype(jnp.bfloat16), 'dp', scatter_dimensio...  32 us
    slice x15, local copies, waits for them, and re-layouts, split_heads(): sliced = source[..., column:column + head_block]  29.6 us
    unnamed x158, local copies, waits for them, and re-layouts  21.5 us
  transfers between devices with their start and end apart: 10, of which 7 were waited for; matrix products, arithmetic and copies ran while one was open for 15% of the time, Pallas kernels for 0%

profile of v1, /device:TPU:0, one launch (start us, length us, event | category | flops | bytes accessed | tf_op | source)
XLA Modules:
  0.0 629.9 jit_solution(2256394956460347064)
XLA Ops:
  11.5 3.3 fusion.25
  17.7 2.0 fusion.106
  27.8 37.6 %all-gather.2.cloned.1.call-done = bf16[1,1024,1536]{2,1,0:T(8,128)(2,1)} async-done(((bf16[1,512,1536]{2,1,0:T(8,128)(2,1)}), bf16[1,1024,1536]{2,1,0:T(8,128)(2,1)}) %all-gather.2.cloned.1.call-update) | async-done | bytes 3145744 | tf_op jit(solution)/shard_map/all_gather | solution.py:62
  65.4 3.5 fusion.105
  69.0 2.0 copy.71
  71.0 2.0 copy.77
  73.1 2.1 copy.75
  75.1 2.0 copy.74
  77.2 2.0 copy.72
  79.2 2.1 copy.69
  81.3 3.1 fusion.110
  84.4 2.0 fusion.1
  86.5 2.1 fusion.80
  92.4 2.1 fusion.81
  99.5 2.1 fusion.79
  101.9 2.0 fusion.103
  104.3 21.1 %multiply_convert_fusion.3 = (bf16[512,3072]{1,0:T(8,128)(2,1)}, f32[512,3072]{1,0:T(8,128)}, f32[512,3072]{1,0:T(8,128)}) fusion(f32[3072]{0:T(1024)S(1)} %copy-done.61, bf16[768,3072]{1,0:T(8,128)(2,1)S(1)} %bitcast.237, f32[512,768]{1,0:T(8,128)S(1)} %get-tuple-element.58, f32[768]{0:T(1024)S(1)} %copy-done.63, f32[768]{0:T(1024)S(1)} %copy-done.58, ...), kind=kOutput, calls=%fused_computation.28 | convolution fusion | flops 2521694208 | bytes 22042624 | tf_op jit(solution)/shard_map/dot_general | solution.py:101
  125.4 8.6 %convert_reduce_fusion = (f32[3072]{0:T(1024)}, bf16[512,3072]{1,0:T(8,128)(2,1)S(1)}) fusion(f32[512,3072]{1,0:T(8,128)} %get-tuple-element.56, bf16[3072,768]{1,0:T(8,128)(2,1)S(1)} %bitcast.239, bf16[1,512,768]{2,1,0:T(8,128)(2,1)S(1)} %copy-done.23, f32[512,3072]{1,0:T(8,128)} %get-tuple-element.83, f32[3072]{0:T(1024)S(1)} %copy-done.61), kind=kOutput, calls=%fused_computation.26 | convolution fusion | flops 2442654720 | bytes 21258240 | tf_op jit(solution)/shard_map/nd,fd->nf/dot_general | solution.py:115
  134.0 2.7 fusion.112
  137.1 4.8 fusion.44
  147.3 2.3 fusion.57
  152.3 5.7 fusion.67
  158.1 7.0 %multiply_reduce_fusion.2 = (f32[4,512]{1,0:T(4,128)}, f32[4,512,1024]{2,1,0:T(8,128)}) fusion(f32[4,512,1024]{2,1,0:T(8,128)} %copy-done.3, f32[4,512]{1,0:T(4,128)S(1)} %copy-done.39, bf16[512,4,64]{0,2,1:T(8,128)(2,1)S(1)} %bitcast.212, bf16[1024,4,64]{0,2,1:T(8,128)(2,1)S(1)} %bitcast.223), kind=kOutput, calls=%fused_computation.8 | convolution fusion | flops 274724864 | bytes 17580032 | tf_op jit(solution)/shard_map/sqhe,skhe->shqk/dot_general | solution.py:150
  166.9 5.8 fusion.61
  172.7 7.2 %multiply_reduce_fusion = (f32[4,512]{1,0:T(4,128)}, f32[4,512,1024]{2,1,0:T(8,128)}) fusion(f32[4,512,1024]{2,1,0:T(8,128)} %copy-done.2, f32[4,512]{1,0:T(4,128)S(1)} %log_add_fusion, bf16[512,4,64]{0,2,1:T(8,128)(2,1)S(1)} %bitcast.214, bf16[1024,4,64]{0,2,1:T(8,128)(2,1)S(1)} %bitcast.221), kind=kOutput, calls=%fused_computation.2 | convolution fusion | flops 274724864 | bytes 17580032 | tf_op jit(solution)/shard_map/sqhe,skhe->shqk/dot_general | solution.py:150
  181.7 5.8 fusion.64
  187.5 7.0 %multiply_reduce_fusion.1 = (f32[4,512]{1,0:T(4,128)}, f32[4,512,1024]{2,1,0:T(8,128)}) fusion(f32[4,512,1024]{2,1,0:T(8,128)} %copy-done.1, f32[4,512]{1,0:T(4,128)S(1)} %log_add_fusion.1, bf16[512,4,64]{0,2,1:T(8,128)(2,1)S(1)} %bitcast.216, bf16[1024,4,64]{0,2,1:T(8,128)(2,1)S(1)} %bitcast.219), kind=kOutput, calls=%fused_computation.5 | convolution fusion | flops 274724864 | bytes 17580032 | tf_op jit(solution)/shard_map/sqhe,skhe->shqk/dot_general | solution.py:150
  194.6 7.0 %multiply_convert_fusion.2 = bf16[4,512,1024]{2,1,0:T(8,128)(2,1)S(1)} fusion(f32[4,512,1024]{2,1,0:T(8,128)} %get-tuple-element.89, f32[4,512,1024]{2,1,0:T(8,128)} %copy-done.3, f32[4,512]{1,0:T(4,128)} %get-tuple-element.88, f32[4,512]{1,0:T(4,128)} %log_add_fusion.2), kind=kLoop, calls=%fused_computation.7 | loop fusion | flops 8388608 | bytes 20987904 | tf_op jit(solution)/shard_map/convert_element_type | solution.py:154
  204.5 4.9 multiply_convert_fusion
  212.3 4.4 multiply_convert_fusion.1
  220.7 32.0 %reduce-scatter.20.cloned.1.call-done = bf16[48,768]{1,0:T(8,128)(2,1)} async-done(((bf16[768,768]{1,0:T(8,128)(2,1)}), bf16[48,768]{1,0:T(8,128)(2,1)}) %reduce-scatter.20.cloned.1.call-update) | async-done | bytes 73744 | tf_op jit(solution)/shard_map/reduce_scatter | solution.py:224
  254.5 7.2 %convolution_convert_fusion = bf16[3072,768]{1,0:T(8,128)(2,1)} fusion(bf16[512,3072]{1,0:T(8,128)(2,1)} %get-tuple-element.55, bf16[1,512,768]{2,1,0:T(8,128)(2,1)} %param.33), kind=kOutput, calls=%fused_computation.42 | convolution fusion | flops 2418278400 | bytes 8650752 | tf_op jit(solution)/shard_map/nf,nd->fd/dot_general | solution.py:113
  262.4 7.4 %convolution_convert_fusion.1 = bf16[768,3072]{1,0:T(8,128)(2,1)} fusion(bf16[512,3072]{1,0:T(8,128)(2,1)} %copy-done.66, f32[512,768]{1,0:T(8,128)} %copy-done.11, f32[768]{0:T(1024)S(1)} %copy-done.64, f32[768]{0:T(1024)S(1)} %copy-done.59, f32[512]{0:T(512)S(1)} %copy-done.56, f32[512]{0:T(512)S(1)} %copy-done.49), kind=kOutput, calls=%fused_computation.43 | convolution fusion | flops 2420244480 | bytes 9447424 | tf_op jit(solution)/shard_map/nd,nf->df/dot_general | solution.py:120
  269.9 3.9 fusion.78
  273.9 2.6 fusion.76
  278.9 18.5 %reduce-scatter.16.cloned.1.call-done = bf16[1,512,1536]{1,2,0:T(8,128)(2,1)} async-done(((bf16[1,1024,1536]{1,2,0:T(8,128)(2,1)}), bf16[1,512,1536]{1,2,0:T(8,128)(2,1)}) %reduce-scatter.16.cloned.1.call-update) | async-done | bytes 1572880 | tf_op jit(solution)/shard_map/reduce_scatter | solution.py:179
  297.4 6.0 convolution_convert_fusion.2
  303.4 7.7 %reduce-scatter.30.cloned.1.call-done = bf16[384,48]{1,0:T(8,128)(2,1)} async-done(((bf16[768,48]{1,0:T(8,128)(2,1)}), bf16[384,48]{1,0:T(8,128)(2,1)}) %reduce-scatter.30.cloned.1.call-update) | async-done | bytes 36880
  314.1 76.8 %reduce-scatter.26.cloned.1.call-done = bf16[192,768]{1,0:T(8,128)(2,1)} async-done(((bf16[3072,768]{1,0:T(8,128)(2,1)}), bf16[192,768]{1,0:T(8,128)(2,1)}) %reduce-scatter.26.cloned.1.call-update) | async-done | bytes 294928 | tf_op jit(solution)/shard_map/reduce_scatter | solution.py:230
  392.8 5.6 fusion.98
  401.0 68.2 %reduce-scatter.22.cloned.1.call-done = bf16[48,3072]{1,0:T(8,128)(2,1)} async-done(((bf16[768,3072]{1,0:T(8,128)(2,1)}), bf16[48,3072]{1,0:T(8,128)(2,1)}) %reduce-scatter.22.cloned.1.call-update) | async-done | bytes 294928 | tf_op jit(solution)/shard_map/reduce_scatter | solution.py:227
  469.5 2.0 convert_reduce_fusion.1
  471.5 3.9 stack.23
  476.1 4.8 convert_reduce_fusion.2
  480.9 59.8 %reduce-scatter.18.cloned.1.call-done = bf16[48,2304]{1,0:T(8,128)(2,1)} async-done(((bf16[768,2304]{1,0:T(8,128)(2,1)}), bf16[48,2304]{1,0:T(8,128)(2,1)}) %reduce-scatter.18.cloned.1.call-update) | async-done | bytes 221200 | tf_op jit(solution)/shard_map/reduce_scatter | solution.py:221
  540.7 2.0 copy.81
  543.3 10.6 %all-reduce.1 = (f32[768]{0:T(1024)}, f32[768]{0:T(1024)}, f32[768]{0:T(1024)}, f32[768]{0:T(1024)}, f32[768]{0:T(1024)}, /*index=5*/f32[768]{0:T(1024)}, f32[76...) all-reduce(f32[768]{0:T(1024)} %get-tuple-element.18, ...), channel_id=1, replica_groups=mesh['dp'=16,'tile'=2] {'tile'}, use_global_device_ids=true, to_apply=%region_19.20 | all-reduce | flops 9221 | bytes 73768 | tf_op jit(solution)/shard_map/psum | solution.py:203
  553.9 58.8 %all-reduce = (f32[768]{0:T(1024)}, f32[768]{0:T(1024)}, f32[768]{0:T(1024)}, f32[768]{0:T(1024)}, f32[768]{0:T(1024)}, /*index=5*/f32[768]{0:T(1024)}, f32[768]...) all-reduce(f32[768]{0:T(1024)} %get-tuple-element.39, ...), channel_id=1, replica_groups=mesh['dp'=16,'tile'=2] {'dp'}, use_global_device_ids=true, to_apply=%region_20.21 | all-reduce | flops 9221 | bytes 73768 | tf_op jit(solution)/shard_map/psum | solution.py:218
  (237 shorter events, 69.5 us)
Async XLA Ops:
  7.2 4.3 copy-start
  7.2 58.2 %all-gather.2.cloned.1.call-start = ((), (), s32[]{:S(2)}) async-start(), calls=%async_computation.9 | async-start | bytes 4718592 | tf_op jit(solution)/shard_map/all_gather | solution.py:62
  8.7 6.1 copy-start.42
  10.2 4.6 copy-start.45
  16.3 8.8 %copy-start.53 = (s32[1,1024]{1,0:T(1,128)S(1)}, s32[1,1024]{1,0:T(1,128)}, u32[]{:S(2)}) copy-start(s32[1,1024]{1,0:T(1,128)} %param.18) | copy-start | bytes 12292
  16.3 8.8 %copy-start.54 = (s32[1,1024]{1,0:T(1,128)S(1)}, s32[1,1024]{1,0:T(1,128)}, u32[]{:S(2)}) copy-start(s32[1,1024]{1,0:T(1,128)} %param.19) | copy-start | bytes 12292
  17.6 235.1 %reduce-scatter.20.cloned.1.call-start = ((), (), s32[]{:S(2)}) async-start(), calls=%async_computation.12 | async-start | bytes 1253376 | tf_op jit(solution)/shard_map/reduce_scatter | solution.py:224
  84.4 4.3 copy-start.1
  90.5 4.1 copy-start.2
  96.4 5.3 copy-start.3
  99.5 4.7 slice-start.4
  99.5 4.7 slice-start.5
  101.9 23.5 %slice-start.6 = ((s8[4718592]{0:T(1024)(128)(4,1)}), s8[4194304]{0:T(1024)(128)(4,1)S(1)}, s32[]{:S(2)}) async-start(s8[4718592]{0:T(1024)(128)(4,1)} %bitcast.238), calls=%async_computation.25 | async-start | bytes 8388608
  103.9 38.0 %copy-start.11 = (f32[512,768]{1,0:T(8,128)}, f32[512,768]{1,0:T(8,128)S(1)}, u32[]{:S(2)}) copy-start(f32[512,768]{1,0:T(8,128)S(1)} %get-tuple-element.58) | copy-start | bytes 4718596
  103.9 38.0 %copy-start.48 = (f32[512]{0:T(512)}, f32[512]{0:T(512)S(1)}, u32[]{:S(2)}) copy-start(f32[512]{0:T(512)S(1)} %broadcast_multiply_fusion) | copy-start | bytes 6148
  104.3 37.7 %copy-start.55 = (f32[512]{0:T(512)}, f32[512]{0:T(512)S(1)}, u32[]{:S(2)}) copy-start(f32[512]{0:T(512)S(1)} %fusion.91) | copy-start | bytes 6148
  104.3 21.1 %copy-start.23 = (bf16[1,512,768]{2,1,0:T(8,128)(2,1)S(1)}, bf16[1,512,768]{2,1,0:T(8,128)(2,1)}, u32[]{:S(2)}) copy-start(bf16[1,512,768]{2,1,0:T(8,128)(2,1)} %param.33) | copy-start | bytes 2359300
  104.3 21.1 %slice-start.7 = ((s8[4718592]{0:T(1024)(128)(4,1)}), s8[524288]{0:T(1024)(128)(4,1)S(1)}, s32[]{:S(2)}) async-start(s8[4718592]{0:T(1024)(128)(4,1)} %bitcast.238), calls=%async_computation.26 | async-start | bytes 1048576
  152.3 5.7 copy-start.24
  152.3 5.7 copy-start.33
  152.3 5.7 copy-start.39
  166.9 5.8 copy-start.25
  166.9 5.8 copy-start.31
  181.7 5.8 copy-start.26
  181.7 5.8 copy-start.29
  194.6 102.8 %reduce-scatter.16.cloned.1.call-start = ((), (), s32[]{:S(2)}) async-start(), calls=%async_computation.10 | async-start | bytes 4718592 | tf_op jit(solution)/shard_map/reduce_scatter | solution.py:179
  194.6 9.1 %slice-start.2 = ((s8[8388608]{0:T(1024)(128)(4,1)}), s8[4194304]{0:T(1024)(128)(4,1)S(1)}, s32[]{:S(2)}) async-start(s8[8388608]{0:T(1024)(128)(4,1)} %bitcast.190), calls=%async_computation.21 | async-start | bytes 8388608
  194.6 7.0 %copy-start.22 = (bf16[1,512,256]{1,2,0:T(8,128)(2,1)S(1)}, bf16[1,512,256]{1,2,0:T(8,128)(2,1)}, u32[]{:S(2)}) copy-start(bf16[1,512,256]{1,2,0:T(8,128)(2,1)} %copy.70) | copy-start | bytes 786436
  194.6 9.8 %slice-start.3 = ((s8[8388608]{0:T(1024)(128)(4,1)}), s8[4194304]{0:T(1024)(128)(4,1)S(1)}, s32[]{:S(2)}) async-start(s8[8388608]{0:T(1024)(128)(4,1)} %bitcast.190), calls=%async_computation.22 | async-start | bytes 8388608
  203.7 8.5 %slice-start = ((s8[8388608]{0:T(1024)(128)(4,1)}), s8[4194304]{0:T(1024)(128)(4,1)S(1)}, s32[]{:S(2)}) async-start(s8[8388608]{0:T(1024)(128)(4,1)} %bitcast.188), calls=%async_computation.19 | async-start | bytes 8388608
  204.4 4.9 copy-start.20
  204.5 7.8 %slice-start.1 = ((s8[8388608]{0:T(1024)(128)(4,1)}), s8[4194304]{0:T(1024)(128)(4,1)S(1)}, s32[]{:S(2)}) async-start(s8[8388608]{0:T(1024)(128)(4,1)} %bitcast.188), calls=%async_computation.20 | async-start | bytes 8388608
  212.2 4.4 copy-start.18
  220.6 90.5 %reduce-scatter.30.cloned.1.call-start = ((), (), s32[]{:S(2)}) async-start(), calls=%async_computation.17 | async-start | bytes 294912
  254.4 136.4 %reduce-scatter.26.cloned.1.call-start = ((), (), s32[]{:S(2)}) async-start(), calls=%async_computation.15 | async-start | bytes 5013504 | tf_op jit(solution)/shard_map/reduce_scatter | solution.py:230
  261.7 207.4 %reduce-scatter.22.cloned.1.call-start = ((), (), s32[]{:S(2)}) async-start(), calls=%async_computation.13 | async-start | bytes 5013504 | tf_op jit(solution)/shard_map/reduce_scatter | solution.py:227
  269.8 270.9 %reduce-scatter.18.cloned.1.call-start = ((), (), s32[]{:S(2)}) async-start(), calls=%async_computation.11 | async-start | bytes 3760128 | tf_op jit(solution)/shard_map/reduce_scatter | solution.py:221
  269.9 6.7 %copy-start.8 = (bf16[4,512,1024]{2,1,0:T(8,128)(2,1)S(1)}, bf16[4,512,1024]{2,1,0:T(8,128)(2,1)}, u32[]{:S(2)}) copy-start(bf16[4,512,1024]{2,1,0:T(8,128)(2,1)} %copy-done.7) | copy-start | bytes 12582916
  269.9 6.6 %copy-start.17 = (bf16[1,1024,256]{1,2,0:T(8,128)(2,1)S(1)}, bf16[1,1024,256]{1,2,0:T(8,128)(2,1)}, u32[]{:S(2)}) copy-start(bf16[1,1024,256]{1,2,0:T(8,128)(2,1)} %copy.74) | copy-start | bytes 1572868
  273.8 23.5 %copy-start.43 = (f32[512]{0:T(512)S(1)}, f32[512]{0:T(512)}, u32[]{:S(2)}) copy-start(f32[512]{0:T(512)} %copy-done.42) | copy-start | bytes 6148
  273.9 23.5 %copy-start.46 = (f32[512]{0:T(512)S(1)}, f32[512]{0:T(512)}, u32[]{:S(2)}) copy-start(f32[512]{0:T(512)} %copy-done.45) | copy-start | bytes 6148
  273.9 23.5 %copy-start.52 = (f32[768]{0:T(1024)S(1)}, f32[768]{0:T(1024)}, u32[]{:S(2)}) copy-start(f32[768]{0:T(1024)} %param.20) | copy-start | bytes 9220
  273.9 23.5 %copy-start.65 = (f32[768]{0:T(1024)S(1)}, f32[768]{0:T(1024)}, u32[]{:S(2)}) copy-start(f32[768]{0:T(1024)} %param.21) | copy-start | bytes 9220
  303.4 311.1 %reduce-scatter.32.cloned.1.call-start = ((), (), s32[]{:S(2)}) async-start(), calls=%async_computation.18 | async-start | bytes 589824
  392.8 225.1 %reduce-scatter.24.cloned.1.call-start = ((), (), s32[]{:S(2)}) async-start(), calls=%async_computation.14 | async-start | bytes 442368 | tf_op jit(solution)/shard_map/reduce_scatter | solution.py:241
  392.8 5.6 copy-start.51
  392.8 6.8 %copy-start.10 = (bf16[1,512,768]{2,1,0:T(8,128)(2,1)S(1)}, bf16[1,512,768]{2,1,0:T(8,128)(2,1)}, u32[]{:S(2)}) copy-start(bf16[1,512,768]{2,1,0:T(8,128)(2,1)} %param.17) | copy-start | bytes 2359300
  469.2 150.3 %reduce-scatter.28.cloned.1.call-start = ((), (), s32[]{:S(2)}) async-start(), calls=%async_computation.16 | async-start | bytes 884736
  (38 other events, 77.4 us)
Sparse Core Ops, SparseCore 0:
  17.8 47.6 all-gather.1
  194.7 57.9 reduce-scatter.19
  254.9 42.3 reduce-scatter.15
  300.1 10.9 reduce-scatter.29
  315.3 75.5 reduce-scatter.25
  394.6 74.5 reduce-scatter.21
  473.5 67.0 reduce-scatter.17
  543.0 12.1 reduce-scatter.31
  557.4 12.0 reduce-scatter.23
  571.6 15.2 reduce-scatter.27
